TPU v7x, 512 devices: a whole 4x4x16 slice. The times are simulated.
512 devices in a mesh: gx: 64 (over z, y), gz: 8 (over x, core).
Axes of the slice: x: 4, y: 4, z: 16, core: 2. Of those that a mesh axis runs over, the one named last changes fastest.
Arguments:
- tokens: bfloat16 [4, 256, 64, 768], P(None, 'gx', 'gz'), may hold values from -60 to 60
- cross_qkv: bfloat16 [768, 2304], P(None, 'gx'), may hold values from -16 to 16
- cross_out: bfloat16 [768, 768], P('gx'), may hold values from -0.21875 to 0.21875
- depth_qkv: bfloat16 [768, 2304], P(None, 'gx'), may hold values from -16 to 16
- depth_out: bfloat16 [768, 768], P('gx'), may hold values from -0.21875 to 0.21875
- up_proj: bfloat16 [768, 3072], P(None, 'gz'), may hold values from -0.21875 to 0.21875
- down_proj: bfloat16 [3072, 768], P('gz'), may hold values from -0.109375 to 0.109375
- gains: float32 [3, 768], replicated, may hold values from 0.5 to 1.5
- head_weight: float32 [768], replicated, may hold values from -0.21875 to 0.21875
- head_bias: float32 [1], replicated, may hold values from -1 to 1
Outputs:
- features: bfloat16 [4, 256, 64, 768], P(None, 'gx', 'gz')
- geotime: float32 [4, 256, 64], P(None, 'gx', 'gz')
All inputs are finite; a program needn't handle non-finite values.
Results may differ from a plain program's by a relative error of at most 0.013.
Values may be sent and summed in bfloat16 or wider, within the bound.
A program may use at most 64 MiB of HBM per device.

v0:
```python
import math
import jax
import jax.numpy as jnp
from jax import lax
from jax.sharding import PartitionSpec as P

HDIM = 64
log_span = math.log(256.0)


def carried_in(shard, axis, combine, identity):
    peers, position = (lax.axis_size(axis), lax.axis_index(axis))
    everything = lax.all_gather(shard, axis)
    start = jnp.broadcast_to(jnp.asarray(identity, shard.dtype), shard.shape)

    def step(k, before):
        reached = k < position
        new = combine(before, everything[k])
        return jnp.where(reached, new, before)

    return lax.fori_loop(0, peers, step, start)


def encodings(inlines, crosslines, depths, cross_start, depth_start, model_width):
    pairs = model_width // 2
    index = jnp.arange(pairs)
    freq = math.pi * jnp.exp(-log_span * index.astype(jnp.float32) / pairs)
    which = index % 3
    inline_pos = jnp.arange(inlines).astype(jnp.float32)[:, None, None, None]
    cross_pos = (cross_start + jnp.arange(crosslines)).astype(jnp.float32)[None, :, None, None]
    depth_pos = (depth_start + jnp.arange(depths)).astype(jnp.float32)[None, None, :, None]
    zeros = jnp.zeros((inlines, crosslines, depths, pairs), jnp.float32)
    position = jnp.where(
        which == 0, inline_pos + zeros, jnp.where(which == 1, cross_pos + zeros, depth_pos + zeros)
    )
    angle = position * freq
    return jnp.stack([jnp.sin(angle), jnp.cos(angle)], -1).reshape(
        inlines, crosslines, depths, model_width
    )


def normalize(stream, gain):
    scale = lax.rsqrt(jnp.mean(stream * stream, -1, keepdims=True) + 1e-05)
    return (stream * scale * gain).astype(jnp.bfloat16)


def attend(queries, keys, values):
    scale = queries.shape[-1] ** (-0.5)
    scores = (
        jnp.einsum("...qe,...ke->...qk", queries, keys, preferred_element_type=jnp.float32) * scale
    )
    scores = scores - jnp.max(scores, -1, keepdims=True)
    expo = jnp.exp(scores)
    weights = (expo / jnp.sum(expo, -1, keepdims=True)).astype(jnp.bfloat16)
    mixed = jnp.einsum("...qk,...ke->...qe", weights, values, preferred_element_type=jnp.float32)
    return mixed.astype(jnp.bfloat16)


def attend_items(trio):
    return attend(trio[0], trio[1], trio[2])


def body(
    tokens,
    cross_qkv,
    cross_out,
    depth_qkv,
    depth_out,
    up_proj,
    down_proj,
    gains,
    head_weight,
    head_bias,
):
    inlines, cross_dev, depth_dev, model_width = tokens.shape
    tok_rows = inlines * cross_dev * depth_dev
    head_count = model_width // HDIM
    cross_group = lax.axis_size("gx")
    encoding = encodings(
        inlines,
        cross_dev,
        depth_dev,
        lax.axis_index("gx") * cross_dev,
        lax.axis_index("gz") * depth_dev,
        model_width,
    )
    stream = (tokens.astype(jnp.float32) + encoding).reshape(tok_rows, model_width)
    normed = normalize(stream, gains[0])
    packed = jnp.dot(
        normed,
        lax.all_gather(cross_qkv, "gx", axis=1, tiled=True),
        preferred_element_type=jnp.float32,
    ).astype(jnp.bfloat16)
    packed = packed.reshape(inlines, cross_dev, depth_dev, 3, head_count, HDIM)
    lined = jnp.transpose(packed, (3, 0, 2, 4, 1, 5))
    per_item = inlines * depth_dev * head_count // cross_group
    lined = lined.reshape(3, cross_group, per_item, cross_dev, HDIM)
    mixed = attend_items(
        (
            lax.all_to_all(lined[0], "gx", split_axis=0, concat_axis=2, tiled=True),
            lax.all_to_all(lined[1], "gx", split_axis=0, concat_axis=2, tiled=True),
            lax.all_to_all(lined[2], "gx", split_axis=0, concat_axis=2, tiled=True),
        )
    )
    mixed = lax.all_to_all(mixed, "gx", split_axis=2, concat_axis=0, tiled=True)
    mixed = jnp.transpose(
        mixed.reshape(inlines, depth_dev, head_count, cross_dev, HDIM), (0, 3, 1, 2, 4)
    ).reshape(tok_rows, model_width)
    columns = mixed
    stream = stream + jnp.dot(
        columns,
        lax.all_gather(cross_out, "gx", axis=0, tiled=True),
        preferred_element_type=jnp.float32,
    )
    normed = normalize(stream, gains[1])
    packed = jnp.dot(
        normed,
        lax.all_gather(depth_qkv, "gx", axis=1, tiled=True),
        preferred_element_type=jnp.float32,
    ).astype(jnp.bfloat16)
    packed = packed.reshape(inlines, cross_dev, depth_dev, 3, head_count, HDIM)
    lined = jnp.transpose(packed, (3, 0, 1, 4, 2, 5))
    all_keys, all_values = (
        lax.all_gather(lined[1], "gz", axis=3, tiled=True),
        lax.all_gather(lined[2], "gz", axis=3, tiled=True),
    )
    mixed = attend(lined[0], all_keys, all_values)
    mixed = jnp.transpose(mixed, (0, 1, 3, 2, 4)).reshape(tok_rows, model_width)
    columns = mixed
    stream = stream + jnp.dot(
        columns,
        lax.all_gather(depth_out, "gx", axis=0, tiled=True),
        preferred_element_type=jnp.float32,
    )
    normed = normalize(stream, gains[2])
    hidden = jax.nn.gelu(
        jnp.dot(
            lax.all_gather(normed, "gz", axis=0, tiled=True),
            up_proj,
            preferred_element_type=jnp.float32,
        )
    ).astype(jnp.bfloat16)
    stream = stream + lax.psum_scatter(
        jnp.dot(hidden, down_proj, preferred_element_type=jnp.float32).astype(jnp.bfloat16),
        "gz",
        scatter_dimension=0,
        tiled=True,
    ).astype(jnp.float32)
    features = stream.astype(jnp.bfloat16).reshape(inlines, cross_dev, depth_dev, model_width)
    thickness = jax.nn.softplus(
        jnp.dot(stream, head_weight, precision=lax.Precision.HIGHEST) + head_bias[0]
    )
    local_time = jnp.cumsum(thickness.reshape(inlines, cross_dev, depth_dev), axis=2)
    line_total = local_time[:, :, -1]
    carried = carried_in(
        line_total, "gz", lambda earlier, later: earlier + later, jnp.zeros_like(line_total)
    )
    geotime = local_time + carried[:, :, None]
    return (features, geotime)


def solution(mesh):
    return jax.shard_map(
        body,
        mesh=mesh,
        in_specs=(
            P(None, "gx", "gz", None),
            P(None, "gx"),
            P("gx", None),
            P(None, "gx"),
            P("gx", None),
            P(None, "gz"),
            P("gz", None),
            P(),
            P(),
            P(),
        ),
        out_specs=(P(None, "gx", "gz", None), P(None, "gx", "gz")),
        check_vma=False,
    )
```

profile of v0, /device:TPU:1, one launch (start us, length us, event | category | flops | bytes accessed | tf_op | source)
XLA Modules:
  0.0 772.2 jit_solution(6534772506447443359)
XLA Ops:
  7.2 0.7 all-gather.21.cloned.1.call-update
  8.0 0.7 all-gather.23.cloned.1.call-update
  8.7 0.7 all-gather.25.cloned.1.call-update
  9.5 0.8 fusion.41
  10.3 6.4 copy.57
  16.6 4.4 copy.58
  21.4 132.3 %all-gather.21.cloned.1.call-done = bf16[64,36,768]{2,1,0:T(8,128)(2,1)} async-done(((bf16[1,36,768]{2,1,0:T(8,128)(2,1)}), bf16[64,36,768]{2,1,0:T(8,128)(2,1)}) %all-gather.21.cloned.1.call-update) | async-done | bytes 3538960 | tf_op jit(solution)/shard_map/all_gather | solution.py:91
  153.7 6.2 reshape.159
  159.8 3.3 convolution_convert_fusion.1
  163.1 1.0 reshape.145
  164.1 1.1 fusion.53
  165.3 0.3 copy.61
  165.6 0.9 reshape.175
  166.5 8.7 %all-to-all-start.1 = ((bf16[64,2,768]{2,1,0:T(2,128)(2,1)}), bf16[64,2,768]{2,1,0:T(2,128)(2,1)S(1)}, u32[]{:S(2)}, u32[]{:S(2)}) async-start(bf16[64,2,768]{2,1,0:T(2,128)(2,1)} %reshape.175), calls=%async_computation.1 | async-start | bytes 393216 | tf_op jit(solution)/shard_map/all_to_all | solution.py:101
  175.2 0.3 copy.59
  175.5 0.9 reshape.173
  176.5 15.4 %all-to-all-done.1 = bf16[64,2,768]{2,1,0:T(2,128)(2,1)S(1)} async-done(((bf16[64,2,768]{2,1,0:T(2,128)(2,1)}), bf16[64,2,768]{2,1,0:T(2,128)(2,1)S(1)}, u32[]{:S(2)}, u32[]{:S(2)}) %all-to-all-start.1) | async-done | bytes 196640 | tf_op jit(solution)/shard_map/all_to_all | solution.py:101
  191.9 4.6 all-to-all-start
  196.5 0.3 copy.65
  196.8 0.9 reshape.171
  197.7 15.1 %all-to-all-done = bf16[64,2,768]{2,1,0:T(2,128)(2,1)S(1)} async-done(((bf16[64,2,768]{2,1,0:T(2,128)(2,1)}), bf16[64,2,768]{2,1,0:T(2,128)(2,1)S(1)}, u32[]{:S(2)}, u32[]{:S(2)}) %all-to-all-start) | async-done | bytes 196640 | tf_op jit(solution)/shard_map/all_to_all | solution.py:100
  212.9 4.6 all-to-all-start.2
  217.5 0.5 all-gather.27.cloned.1.call-update
  218.1 0.3 reshape.176
  218.5 0.3 reshape.174
  218.9 15.0 %all-to-all-done.2 = bf16[64,2,768]{2,1,0:T(2,128)(2,1)S(1)} async-done(((bf16[64,2,768]{2,1,0:T(2,128)(2,1)}), bf16[64,2,768]{2,1,0:T(2,128)(2,1)S(1)}, u32[]{:S(2)}, u32[]{:S(2)}) %all-to-all-start.2) | async-done | bytes 196640 | tf_op jit(solution)/shard_map/all_to_all | solution.py:102
  234.4 1.8 fusion.55
  236.2 1.7 fusion.27
  237.9 0.3 copy.69
  238.2 1.0 reshape.177
  239.2 4.6 all-to-all-start.3
  244.1 49.5 %all-gather.23.cloned.1.call-done = bf16[64,12,768]{2,1,0:T(8,128)(2,1)} async-done(((bf16[1,12,768]{2,1,0:T(8,128)(2,1)}), bf16[64,12,768]{2,1,0:T(8,128)(2,1)}) %all-gather.23.cloned.1.call-update) | async-done | bytes 1179664 | tf_op jit(solution)/shard_map/all_gather | solution.py:112
  293.6 2.2 reshape.161
  295.9 142.8 %all-gather.25.cloned.1.call-done = bf16[64,36,768]{2,1,0:T(8,128)(2,1)} async-done(((bf16[1,36,768]{2,1,0:T(8,128)(2,1)}), bf16[64,36,768]{2,1,0:T(8,128)(2,1)}) %all-gather.25.cloned.1.call-update) | async-done | bytes 3538960 | tf_op jit(solution)/shard_map/all_gather | solution.py:118
  438.7 6.2 reshape.163
  444.9 0.3 reshape.178
  445.5 0.3 reshape.150
  445.8 0.4 multiply_reduce_fusion.1
  446.2 0.7 copy-done.1
  447.0 3.3 convolution_convert_fusion
  450.3 1.0 reshape.151
  451.3 0.3 copy.84
  451.6 1.0 fusion.54
  452.6 0.5 all-gather.19.cloned.1.call-update
  453.2 122.6 %all-gather.27.cloned.1.call-done = bf16[64,12,768]{2,1,0:T(8,128)(2,1)} async-done(((bf16[1,12,768]{2,1,0:T(8,128)(2,1)}), bf16[64,12,768]{2,1,0:T(8,128)(2,1)}) %all-gather.27.cloned.1.call-update) | async-done | bytes 1179664 | tf_op jit(solution)/shard_map/all_gather | solution.py:132
  575.8 2.2 reshape.165
  578.1 44.5 %all-gather.17.cloned.1.call-done = bf16[1,4,4,12,64,64]{5,4,3,2,1,0:T(8,128)(2,1)} async-done(((bf16[1,4,4,12,8,64]{5,4,3,2,1,0:T(8,128)(2,1)}), bf16[1,4,4,12,64,64]{5,4,3,2,1,0:T(8,128)(2,1)}) %all-gather.17.cloned.1.call-update) | async-done | bytes 1572880 | tf_op jit(solution)/shard_map/all_gather | solution.py:124
  622.5 4.6 fusion.56
  627.2 37.7 %all-gather.19.cloned.1.call-done = bf16[1,4,4,12,64,64]{5,4,3,2,1,0:T(8,128)(2,1)} async-done(((bf16[1,4,4,12,8,64]{5,4,3,2,1,0:T(8,128)(2,1)}), bf16[1,4,4,12,64,64]{5,4,3,2,1,0:T(8,128)(2,1)}) %all-gather.19.cloned.1.call-update) | async-done | bytes 1572880 | tf_op jit(solution)/shard_map/all_gather | solution.py:125
  664.9 3.1 fusion.24
  668.2 0.3 reshape.152
  668.5 0.6 copy-done.2
  669.0 0.4 multiply_reduce_fusion
  669.5 0.8 multiply_convert_fusion
  670.3 33.1 %all-gather.15.cloned.1.call-done = bf16[1024,768]{1,0:T(8,128)(2,1)} async-done(((bf16[128,768]{1,0:T(8,128)(2,1)}), bf16[1024,768]{1,0:T(8,128)(2,1)}) %all-gather.15.cloned.1.call-update) | async-done | bytes 1572880 | tf_op jit(solution)/shard_map/all_gather | solution.py:138
  703.5 4.6 convolution_convert_fusion.2
  708.2 0.7 copy-done.6
  709.5 37.5 %reduce-scatter.2.cloned.1.call-done = bf16[128,768]{1,0:T(8,128)(2,1)} async-done(((bf16[1024,768]{1,0:T(8,128)(2,1)}), bf16[128,768]{1,0:T(8,128)(2,1)}) %reduce-scatter.2.cloned.1.call-update) | async-done | bytes 196624 | tf_op jit(solution)/shard_map/reduce_scatter | solution.py:143
  747.0 1.4 compare_select_fusion
  748.4 0.7 reduce_window_sum.11
  749.3 13.5 %all-gather.2 = f32[32,4,1]{1,2,0:T(1,128)S(1)} all-gather(f32[4,4,1]{1,2,0:T(1,128)S(1)} %copy.75), channel_id=4, replica_groups=mesh['gx'=64,'gz'=8] {'gz'}, dimensions={0}, use_global_device_ids=true | all-gather | bytes 576 | tf_op jit(solution)/shard_map/all_gather | solution.py:13
  762.8 0.3 while.14
  763.1 0.7 broadcast_add_fusion
  763.8 1.6 fusion.37
  (56 shorter events, 2.5 us)
Async XLA Ops:
  7.2 696.3 %copy-start = (bf16[384,768]{1,0:T(8,128)(2,1)S(1)}, bf16[384,768]{1,0:T(8,128)(2,1)}, u32[]{:S(2)}) copy-start(bf16[384,768]{1,0:T(8,128)(2,1)} %param.18) | copy-start | bytes 1769476
  7.2 146.5 %all-gather.21.cloned.1.call-start = ((), (), s32[]{:S(2)}) async-start(), calls=%async_computation.9 | async-start | bytes 3993600 | tf_op jit(solution)/shard_map/all_gather | solution.py:91
  7.9 285.7 %all-gather.23.cloned.1.call-start = ((), (), s32[]{:S(2)}) async-start(), calls=%async_computation.10 | async-start | bytes 1597440 | tf_op jit(solution)/shard_map/all_gather | solution.py:112
  8.7 430.0 %all-gather.25.cloned.1.call-start = ((), (), s32[]{:S(2)}) async-start(), calls=%async_computation.11 | async-start | bytes 3993600 | tf_op jit(solution)/shard_map/all_gather | solution.py:118
  16.6 4.4 copy-start.4
  16.6 4.6 copy-start.5
  165.2 10.0 %copy-start.3 = (bf16[1,4,8,12,4,64]{5,3,0,2,4,1:T(8,128)(2,1)S(1)}, bf16[1,4,8,12,4,64]{5,3,0,2,4,1:T(8,128)(2,1)}, u32[]{:S(2)}) copy-start(bf16[1,4,8,12,4,64]{5,3,0,2,4,1:T(8,128)(2,1)} %get-tuple-element.128) | copy-start | bytes 589828
  166.5 25.4 %all-to-all-start.1 = ((bf16[64,2,768]{2,1,0:T(2,128)(2,1)}), bf16[64,2,768]{2,1,0:T(2,128)(2,1)S(1)}, u32[]{:S(2)}, u32[]{:S(2)}) async-start(bf16[64,2,768]{2,1,0:T(2,128)(2,1)} %reshape.175), calls=%async_computation.1 | async-start | bytes 393216 | tf_op jit(solution)/shard_map/all_to_all | solution.py:101
  191.9 21.0 %all-to-all-start = ((bf16[64,2,768]{2,1,0:T(2,128)(2,1)}), bf16[64,2,768]{2,1,0:T(2,128)(2,1)S(1)}, u32[]{:S(2)}, u32[]{:S(2)}) async-start(bf16[64,2,768]{2,1,0:T(2,128)(2,1)} %reshape.173), calls=%async_computation | async-start | bytes 393216 | tf_op jit(solution)/shard_map/all_to_all | solution.py:100
  212.9 21.1 %all-to-all-start.2 = ((bf16[64,2,768]{2,1,0:T(2,128)(2,1)}), bf16[64,2,768]{2,1,0:T(2,128)(2,1)S(1)}, u32[]{:S(2)}, u32[]{:S(2)}) async-start(bf16[64,2,768]{2,1,0:T(2,128)(2,1)} %reshape.171), calls=%async_computation.2 | async-start | bytes 393216 | tf_op jit(solution)/shard_map/all_to_all | solution.py:102
  217.5 358.3 %all-gather.27.cloned.1.call-start = ((), (), s32[]{:S(2)}) async-start(), calls=%async_computation.12 | async-start | bytes 1597440 | tf_op jit(solution)/shard_map/all_gather | solution.py:132
  239.2 205.6 %all-to-all-start.3 = ((bf16[64,2,768]{2,1,0:T(2,128)(2,1)}), bf16[64,2,768]{2,1,0:T(2,128)(2,1)S(1)}, u32[]{:S(2)}, u32[]{:S(2)}) async-start(bf16[64,2,768]{2,1,0:T(2,128)(2,1)} %reshape.177), calls=%async_computation.3 | async-start | bytes 393216 | tf_op jit(solution)/shard_map/all_to_all | solution.py:105
  243.9 378.7 %all-gather.17.cloned.1.call-start = ((), (), s32[]{:S(2)}) async-start(), calls=%async_computation.7 | async-start | bytes 3538944 | tf_op jit(solution)/shard_map/all_gather | solution.py:124
  446.2 0.7 copy-start.1
  452.6 212.3 %all-gather.19.cloned.1.call-start = ((), (), s32[]{:S(2)}) async-start(), calls=%async_computation.8 | async-start | bytes 3538944 | tf_op jit(solution)/shard_map/all_gather | solution.py:125
  453.2 250.3 %all-gather.15.cloned.1.call-start = ((), (), s32[]{:S(2)}) async-start(), calls=%async_computation.5 | async-start | bytes 1769472 | tf_op jit(solution)/shard_map/all_gather | solution.py:138
  668.0 1.0 copy-start.2
  670.3 76.7 %reduce-scatter.2.cloned.1.call-start = ((), (), s32[]{:S(2)}) async-start(), calls=%async_computation.6 | async-start | bytes 1769472 | tf_op jit(solution)/shard_map/reduce_scatter | solution.py:143
  708.1 0.7 copy-start.6
Sparse Core Ops, SparseCore 0:
  11.0 142.6 all-gather.20
  156.6 136.9 all-gather.22
  296.6 142.0 all-gather.24
  441.5 134.2 all-gather.26
  577.8 44.7 all-gather.16
  624.5 40.3 all-gather.18
  670.4 33.0 all-gather.14
  708.3 38.6 reduce-scatter.1
where the time goes:
time: 773 us; the launch traced here: 772 us
  waiting for transfers between devices  649 us (84%)
  local copies, waits for them, and re-layouts  41.9 us (5%)
  matrix products  24.7 us (3%)
  starting transfers between devices  23.1 us (3%)
  between operations  15.2 us (2%)
  blocking collectives  13.5 us (2%)
    all_gather x1, waiting for transfers between devices, body(): lax.all_gather(depth_qkv, 'gx', axis=1, tiled=True)  143 us
    all_gather x1, waiting for transfers between devices, body(): lax.all_gather(cross_qkv, 'gx', axis=1, tiled=True)  132 us
    all_gather x1, waiting for transfers between devices, body(): lax.all_gather(depth_out, 'gx', axis=0, tiled=True)  123 us
    all_gather x1, waiting for transfers between devices, body(): lax.all_gather(cross_out, 'gx', axis=0, tiled=True)  49.5 us
    all_gather x1, waiting for transfers between devices, body(): lax.all_gather(lined[1], 'gz', axis=3, tiled=True)  44.5 us
    all_gather x1, waiting for transfers between devices, body(): lax.all_gather(lined[2], 'gz', axis=3, tiled=True)  37.7 us
    reduce_scatter x1, waiting for transfers between devices, body(): lax.psum_scatter(jnp.dot(hidden, down_proj, preferred_element_type=jnp.fl...  37.5 us
    all_gather x1, waiting for transfers between devices, body(): lax.all_gather(normed, 'gz', axis=0, tiled=True)  33.1 us
  transfers between devices with their start and end apart: 12, of which 11 were waited for; matrix products, arithmetic and copies ran while one was open for 7% of the time, Pallas kernels for 0%

commit v1 on v0

--- a/solution.py
+++ b/solution.py
@@ -6,6 +6,24 @@
 
 HDIM = 64
 log_span = math.log(256.0)
+
+
+def ring_gather(array, axis, dim):
+    ways, here, hop = (lax.axis_size(axis), lax.axis_index(axis), array.shape[dim])
+    lengths = [n * ways if d == dim else n for d, n in enumerate(array.shape)]
+    full = lax.dynamic_update_slice_in_dim(
+        jnp.zeros(lengths, array.dtype), array, here * hop, axis=dim
+    )
+    going_up = going_down = array
+    for far in range(1, ways // 2 + 1):
+        going_up = lax.ppermute(going_up, axis, [(d, (d + 1) % ways) for d in range(ways)])
+        full = lax.dynamic_update_slice_in_dim(full, going_up, (here - far) % ways * hop, axis=dim)
+        if 2 * far < ways:
+            going_down = lax.ppermute(going_down, axis, [(d, (d - 1) % ways) for d in range(ways)])
+            full = lax.dynamic_update_slice_in_dim(
+                full, going_down, (here + far) % ways * hop, axis=dim
+            )
+    return full
 
 
 def carried_in(shard, axis, combine, identity):
@@ -121,7 +139,7 @@
     packed = packed.reshape(inlines, cross_dev, depth_dev, 3, head_count, HDIM)
     lined = jnp.transpose(packed, (3, 0, 1, 4, 2, 5))
     all_keys, all_values = (
-        lax.all_gather(lined[1], "gz", axis=3, tiled=True),
+        ring_gather(lined[1], "gz", 3),
         lax.all_gather(lined[2], "gz", axis=3, tiled=True),
     )
     mixed = attend(lined[0], all_keys, all_values)

time: 773 us -> 735 us (0.951)
  waiting for transfers between devices: 649 us -> 580 us
  starting transfers between devices: 23.1 us -> 44.6 us
  local copies, waits for them, and re-layouts: 41.9 us -> 50.8 us
    all_gather x1 -> x0, waiting for transfers between devices: 44.5 us -> none  [body(): lax.all_gather(lined[1], 'gz', axis=3, tiled=True)]
    all_gather x1, waiting for transfers between devices: 37.7 us -> 2.01 us  [body(): lax.all_gather(lined[2], 'gz', axis=3, tiled=True)]
    ppermute x0 -> x7, starting transfers between devices: none -> 21.6 us  [the longest x4 17.5 us: ring_gather(): lax.ppermute(going_up, axis, [(d, (d + 1) % ways) for d in range(ways)])]
    ppermute x0 -> x7, waiting for transfers between devices: none -> 10.9 us  [the longest x4 6.5 us: ring_gather(): lax.ppermute(going_up, axis, [(d, (d + 1) % ways) for d in range(ways)])]
  transfers between devices with their start and end apart: 12 -> 18, of which waited for: 11 -> 15; matrix products, arithmetic and copies ran while one was open for 7% -> 9% of each run, Pallas kernels for 0% -> 0%
where the time goes in v1:
time: 735 us; the launch traced here: 734 us
  waiting for transfers between devices  580 us (79%)
  local copies, waits for them, and re-layouts  50.8 us (7%)
  starting transfers between devices  44.6 us (6%)
  matrix products  24.7 us (3%)
  between operations  15.3 us (2%)
  blocking collectives  13.4 us (2%)
    all_gather x1, waiting for transfers between devices, body(): lax.all_gather(depth_qkv, 'gx', axis=1, tiled=True)  143 us
    all_gather x1, waiting for transfers between devices, body(): lax.all_gather(cross_qkv, 'gx', axis=1, tiled=True)  132 us
    all_gather x1, waiting for transfers between devices, body(): lax.all_gather(depth_out, 'gx', axis=0, tiled=True)  123 us
    all_gather x1, waiting for transfers between devices, body(): lax.all_gather(cross_out, 'gx', axis=0, tiled=True)  49.9 us
    reduce_scatter x1, waiting for transfers between devices, body(): lax.psum_scatter(jnp.dot(hidden, down_proj, preferred_element_type=jnp.fl...  37.5 us
    all_gather x1, waiting for transfers between devices, body(): lax.all_gather(normed, 'gz', axis=0, tiled=True)  33.2 us
    unnamed x27, local copies, waits for them, and re-layouts  23.8 us
    ppermute x4, starting transfers between devices, ring_gather(): lax.ppermute(going_up, axis, [(d, (d + 1) % ways) for d in range(ways)])  17.5 us
  transfers between devices with their start and end apart: 18, of which 15 were waited for; matrix products, arithmetic and copies ran while one was open for 9% of the time, Pallas kernels for 0%

profile of v1, /device:TPU:1, one launch (start us, length us, event | category | flops | bytes accessed | tf_op | source)
XLA Modules:
  0.0 734.0 jit_solution(8789160817267933397)
XLA Ops:
  7.2 0.7 all-gather.17.cloned.1.call-update
  8.0 0.7 all-gather.19.cloned.1.call-update
  8.7 0.7 all-gather.21.cloned.1.call-update
  9.5 0.8 fusion.36
  10.3 6.3 copy.57
  16.6 4.4 copy.58
  21.4 132.3 %all-gather.17.cloned.1.call-done = bf16[64,36,768]{2,1,0:T(8,128)(2,1)} async-done(((bf16[1,36,768]{2,1,0:T(8,128)(2,1)}), bf16[64,36,768]{2,1,0:T(8,128)(2,1)}) %all-gather.17.cloned.1.call-update) | async-done | bytes 3538960 | tf_op jit(solution)/shard_map/all_gather | solution.py:109
  153.7 6.2 reshape.158
  159.9 3.3 convolution_convert_fusion.1
  163.2 1.0 reshape.145
  164.2 1.1 fusion.48
  165.6 0.9 reshape.174
  166.5 8.7 %all-to-all-start.1 = ((bf16[64,2,768]{2,1,0:T(2,128)(2,1)}), bf16[64,2,768]{2,1,0:T(2,128)(2,1)S(1)}, u32[]{:S(2)}, u32[]{:S(2)}) async-start(bf16[64,2,768]{2,1,0:T(2,128)(2,1)} %reshape.174), calls=%async_computation.1 | async-start | bytes 393216 | tf_op jit(solution)/shard_map/all_to_all | solution.py:119
  175.6 0.9 reshape.172
  176.5 15.4 %all-to-all-done.1 = bf16[64,2,768]{2,1,0:T(2,128)(2,1)S(1)} async-done(((bf16[64,2,768]{2,1,0:T(2,128)(2,1)}), bf16[64,2,768]{2,1,0:T(2,128)(2,1)S(1)}, u32[]{:S(2)}, u32[]{:S(2)}) %all-to-all-start.1) | async-done | bytes 196640 | tf_op jit(solution)/shard_map/all_to_all | solution.py:119
  191.9 4.6 all-to-all-start
  196.8 0.9 reshape.170
  197.7 15.1 %all-to-all-done = bf16[64,2,768]{2,1,0:T(2,128)(2,1)S(1)} async-done(((bf16[64,2,768]{2,1,0:T(2,128)(2,1)}), bf16[64,2,768]{2,1,0:T(2,128)(2,1)S(1)}, u32[]{:S(2)}, u32[]{:S(2)}) %all-to-all-start) | async-done | bytes 196640 | tf_op jit(solution)/shard_map/all_to_all | solution.py:118
  212.9 4.6 all-to-all-start.2
  218.9 15.1 %all-to-all-done.2 = bf16[64,2,768]{2,1,0:T(2,128)(2,1)S(1)} async-done(((bf16[64,2,768]{2,1,0:T(2,128)(2,1)}), bf16[64,2,768]{2,1,0:T(2,128)(2,1)S(1)}, u32[]{:S(2)}, u32[]{:S(2)}) %all-to-all-start.2) | async-done | bytes 196640 | tf_op jit(solution)/shard_map/all_to_all | solution.py:120
  234.5 1.8 fusion.49
  236.3 1.7 fusion.22
  238.3 1.0 reshape.176
  239.3 4.6 all-to-all-start.3
  244.2 49.9 %all-gather.19.cloned.1.call-done = bf16[64,12,768]{2,1,0:T(8,128)(2,1)} async-done(((bf16[1,12,768]{2,1,0:T(8,128)(2,1)}), bf16[64,12,768]{2,1,0:T(8,128)(2,1)}) %all-gather.19.cloned.1.call-update) | async-done | bytes 1179664 | tf_op jit(solution)/shard_map/all_gather | solution.py:130
  294.1 2.2 reshape.160
  296.3 142.7 %all-gather.21.cloned.1.call-done = bf16[64,36,768]{2,1,0:T(8,128)(2,1)} async-done(((bf16[1,36,768]{2,1,0:T(8,128)(2,1)}), bf16[64,36,768]{2,1,0:T(8,128)(2,1)}) %all-gather.21.cloned.1.call-update) | async-done | bytes 3538960 | tf_op jit(solution)/shard_map/all_gather | solution.py:136
  439.0 6.2 reshape.162
  446.6 0.7 copy-done.1
  447.3 3.3 convolution_convert_fusion
  450.6 1.0 reshape.151
  451.9 0.8 slice_bitcast_fusion
  452.9 123.2 %all-gather.23.cloned.1.call-done = bf16[64,12,768]{2,1,0:T(8,128)(2,1)} async-done(((bf16[1,12,768]{2,1,0:T(8,128)(2,1)}), bf16[64,12,768]{2,1,0:T(8,128)(2,1)}) %all-gather.23.cloned.1.call-update) | async-done | bytes 1179664 | tf_op jit(solution)/shard_map/all_gather | solution.py:150
  576.1 2.2 reshape.164
  578.4 11.1 %collective-permute-start = (bf16[4,4,12,8,64]{4,3,2,1,0:T(8,128)(2,1)S(1)}, bf16[4,4,12,8,64]{4,3,2,1,0:T(8,128)(2,1)S(1)}, u32[]{:S(2)}, u32[]{:S(2)}) collective-permute-start(bf16[4,4,12,8,64]{4,3,2,1,0:T(8,128)(2,1)S(1)} %get-tuple-element.129), channel_id=1, source_target_pairs={{0,1},{1,2},{2,3},{3,4},{4,5},{5,6},{6,7},{7,0},{8,9},{9,10},{10,1... | collective-permute-start | bytes 589832 | tf_op jit(solution)/shard_map/ppermute | solution.py:19
  589.5 2.5 broadcast_in_dim.11
  592.0 0.8 constant_dynamic-update-slice_fusion.7
  592.8 1.4 collective-permute-done
  594.2 2.5 collective-permute-start.2
  596.8 0.8 constant_dynamic-update-slice_fusion.6
  597.6 0.8 constant_dynamic-update-slice_fusion.5
  598.5 2.9 collective-permute-done.2
  601.4 2.6 collective-permute-start.4
  604.0 1.4 collective-permute-done.3
  605.4 3.9 collective-permute-start.5
  609.3 0.8 constant_dynamic-update-slice_fusion.4
  610.1 0.8 constant_dynamic-update-slice_fusion.3
  610.9 1.4 collective-permute-start.6
  612.3 0.8 constant_dynamic-update-slice_fusion.2
  613.1 3.0 collective-permute-done.5
  616.2 0.8 constant_dynamic-update-slice_fusion.1
  617.0 2.2 collective-permute-done.6
  619.1 0.8 constant_dynamic-update-slice_fusion
  620.0 4.6 fusion.50
  624.6 2.0 all-gather.15.cloned.1.call-done
  626.6 3.1 fusion.19
  631.2 0.8 multiply_convert_fusion
  632.0 33.2 %all-gather.13.cloned.1.call-done = bf16[1024,768]{1,0:T(8,128)(2,1)} async-done(((bf16[128,768]{1,0:T(8,128)(2,1)}), bf16[1024,768]{1,0:T(8,128)(2,1)}) %all-gather.13.cloned.1.call-update) | async-done | bytes 1572880 | tf_op jit(solution)/shard_map/all_gather | solution.py:156
  665.3 4.7 convolution_convert_fusion.2
  671.3 37.5 %reduce-scatter.2.cloned.1.call-done = bf16[128,768]{1,0:T(8,128)(2,1)} async-done(((bf16[1024,768]{1,0:T(8,128)(2,1)}), bf16[128,768]{1,0:T(8,128)(2,1)}) %reduce-scatter.2.cloned.1.call-update) | async-done | bytes 196624 | tf_op jit(solution)/shard_map/reduce_scatter | solution.py:161
  708.8 1.4 compare_select_fusion
  710.2 0.7 reduce_window_sum.11
  711.1 13.4 %all-gather.1 = f32[32,4,1]{1,2,0:T(1,128)S(1)} all-gather(f32[4,4,1]{1,2,0:T(1,128)S(1)} %copy.75), channel_id=3, replica_groups=mesh['gx'=64,'gz'=8] {'gz'}, dimensions={0}, use_global_device_ids=true | all-gather | bytes 576 | tf_op jit(solution)/shard_map/all_gather | solution.py:31
  725.6 1.6 fusion.32
  (76 shorter events, 9.2 us)
Async XLA Ops:
  7.2 658.1 %copy-start = (bf16[384,768]{1,0:T(8,128)(2,1)S(1)}, bf16[384,768]{1,0:T(8,128)(2,1)}, u32[]{:S(2)}) copy-start(bf16[384,768]{1,0:T(8,128)(2,1)} %param.18) | copy-start | bytes 1769476
  7.2 146.5 %all-gather.17.cloned.1.call-start = ((), (), s32[]{:S(2)}) async-start(), calls=%async_computation.8 | async-start | bytes 3993600 | tf_op jit(solution)/shard_map/all_gather | solution.py:109
  7.9 286.1 %all-gather.19.cloned.1.call-start = ((), (), s32[]{:S(2)}) async-start(), calls=%async_computation.9 | async-start | bytes 1597440 | tf_op jit(solution)/shard_map/all_gather | solution.py:130
  8.7 430.4 %all-gather.21.cloned.1.call-start = ((), (), s32[]{:S(2)}) async-start(), calls=%async_computation.10 | async-start | bytes 3993600 | tf_op jit(solution)/shard_map/all_gather | solution.py:136
  16.6 4.4 copy-start.4
  16.6 4.6 copy-start.5
  165.3 10.0 %copy-start.3 = (bf16[1,4,8,12,4,64]{5,3,0,2,4,1:T(8,128)(2,1)S(1)}, bf16[1,4,8,12,4,64]{5,3,0,2,4,1:T(8,128)(2,1)}, u32[]{:S(2)}) copy-start(bf16[1,4,8,12,4,64]{5,3,0,2,4,1:T(8,128)(2,1)} %get-tuple-element.128) | copy-start | bytes 589828
  166.5 25.4 %all-to-all-start.1 = ((bf16[64,2,768]{2,1,0:T(2,128)(2,1)}), bf16[64,2,768]{2,1,0:T(2,128)(2,1)S(1)}, u32[]{:S(2)}, u32[]{:S(2)}) async-start(bf16[64,2,768]{2,1,0:T(2,128)(2,1)} %reshape.174), calls=%async_computation.1 | async-start | bytes 393216 | tf_op jit(solution)/shard_map/all_to_all | solution.py:119
  191.9 21.0 %all-to-all-start = ((bf16[64,2,768]{2,1,0:T(2,128)(2,1)}), bf16[64,2,768]{2,1,0:T(2,128)(2,1)S(1)}, u32[]{:S(2)}, u32[]{:S(2)}) async-start(bf16[64,2,768]{2,1,0:T(2,128)(2,1)} %reshape.172), calls=%async_computation | async-start | bytes 393216 | tf_op jit(solution)/shard_map/all_to_all | solution.py:118
  212.9 21.2 %all-to-all-start.2 = ((bf16[64,2,768]{2,1,0:T(2,128)(2,1)}), bf16[64,2,768]{2,1,0:T(2,128)(2,1)S(1)}, u32[]{:S(2)}, u32[]{:S(2)}) async-start(bf16[64,2,768]{2,1,0:T(2,128)(2,1)} %reshape.170), calls=%async_computation.2 | async-start | bytes 393216 | tf_op jit(solution)/shard_map/all_to_all | solution.py:120
  217.5 358.6 %all-gather.23.cloned.1.call-start = ((), (), s32[]{:S(2)}) async-start(), calls=%async_computation.11 | async-start | bytes 1597440 | tf_op jit(solution)/shard_map/all_gather | solution.py:150
  239.3 205.9 %all-to-all-start.3 = ((bf16[64,2,768]{2,1,0:T(2,128)(2,1)}), bf16[64,2,768]{2,1,0:T(2,128)(2,1)S(1)}, u32[]{:S(2)}, u32[]{:S(2)}) async-start(bf16[64,2,768]{2,1,0:T(2,128)(2,1)} %reshape.176), calls=%async_computation.3 | async-start | bytes 393216 | tf_op jit(solution)/shard_map/all_to_all | solution.py:123
  243.9 382.7 %all-gather.15.cloned.1.call-start = ((), (), s32[]{:S(2)}) async-start(), calls=%async_computation.7 | async-start | bytes 3538944 | tf_op jit(solution)/shard_map/all_gather | solution.py:143
  446.6 0.7 copy-start.1
  452.8 212.5 %all-gather.13.cloned.1.call-start = ((), (), s32[]{:S(2)}) async-start(), calls=%async_computation.5 | async-start | bytes 1769472 | tf_op jit(solution)/shard_map/all_gather | solution.py:156
  578.4 15.8 %collective-permute-start = (bf16[4,4,12,8,64]{4,3,2,1,0:T(8,128)(2,1)S(1)}, bf16[4,4,12,8,64]{4,3,2,1,0:T(8,128)(2,1)S(1)}, u32[]{:S(2)}, u32[]{:S(2)}) collective-permute-start(bf16[4,4,12,8,64]{4,3,2,1,0:T(8,128)(2,1)S(1)} %get-tuple-element.129), channel_id=1, source_target_pairs={{0,1},{1,2},{2,3},{3,4},{4,5},{5,6},{6,7},{7,0},{8,9},{9,10},{10,1... | collective-permute-start | bytes 589832 | tf_op jit(solution)/shard_map/ppermute | solution.py:19
  589.5 7.2 collective-permute-start.1
  594.2 7.2 collective-permute-start.2
  596.7 8.7 %collective-permute-start.3 = (bf16[4,4,12,8,64]{4,3,2,1,0:T(8,128)(2,1)S(1)}, bf16[4,4,12,8,64]{4,3,2,1,0:T(8,128)(2,1)S(1)}, u32[]{:S(2)}, u32[]{:S(2)}) collective-permute-start(bf16[4,4,12,8,64]{4,3,2,1,0:T(8,128)(2,1)S(1)} %collective-permute-done.1), channel_id=1, source_target_pairs={{0,7},{1,0},{2,1},{3,2},{4,3},{5,4},{6,5},{7,6},{8,15},{9,8},{10,9... | collective-permute-start | bytes 589832 | tf_op jit(solution)/shard_map/ppermute | solution.py:22
  601.4 9.5 %collective-permute-start.4 = (bf16[4,4,12,8,64]{4,3,2,1,0:T(8,128)(2,1)S(1)}, bf16[4,4,12,8,64]{4,3,2,1,0:T(8,128)(2,1)S(1)}, u32[]{:S(2)}, u32[]{:S(2)}) collective-permute-start(bf16[4,4,12,8,64]{4,3,2,1,0:T(8,128)(2,1)S(1)} %collective-permute-done.2), channel_id=1, source_target_pairs={{0,1},{1,2},{2,3},{3,4},{4,5},{5,6},{6,7},{7,0},{8,9},{9,10},{10,1... | collective-permute-start | bytes 589832 | tf_op jit(solution)/shard_map/ppermute | solution.py:19
  605.4 10.8 %collective-permute-start.5 = (bf16[4,4,12,8,64]{4,3,2,1,0:T(8,128)(2,1)S(1)}, bf16[4,4,12,8,64]{4,3,2,1,0:T(8,128)(2,1)S(1)}, u32[]{:S(2)}, u32[]{:S(2)}) collective-permute-start(bf16[4,4,12,8,64]{4,3,2,1,0:T(8,128)(2,1)S(1)} %collective-permute-done.3), channel_id=1, source_target_pairs={{0,7},{1,0},{2,1},{3,2},{4,3},{5,4},{6,5},{7,6},{8,15},{9,8},{10,9... | collective-permute-start | bytes 589832 | tf_op jit(solution)/shard_map/ppermute | solution.py:22
  610.9 8.2 %collective-permute-start.6 = (bf16[4,4,12,8,64]{4,3,2,1,0:T(8,128)(2,1)S(1)}, bf16[4,4,12,8,64]{4,3,2,1,0:T(8,128)(2,1)S(1)}, u32[]{:S(2)}, u32[]{:S(2)}) collective-permute-start(bf16[4,4,12,8,64]{4,3,2,1,0:T(8,128)(2,1)S(1)} %collective-permute-done.4), channel_id=1, source_target_pairs={{0,1},{1,2},{2,3},{3,4},{4,5},{5,6},{6,7},{7,0},{8,9},{9,10},{10,1... | collective-permute-start | bytes 589832 | tf_op jit(solution)/shard_map/ppermute | solution.py:19
  629.7 1.0 copy-start.2
  632.0 76.8 %reduce-scatter.2.cloned.1.call-start = ((), (), s32[]{:S(2)}) async-start(), calls=%async_computation.6 | async-start | bytes 1769472 | tf_op jit(solution)/shard_map/reduce_scatter | solution.py:161
  669.9 0.7 copy-start.6
Sparse Core Ops, SparseCore 0:
  11.0 142.6 all-gather.16
  156.6 137.3 all-gather.18
  297.0 141.9 all-gather.20
  441.8 134.2 all-gather.22
  578.1 48.4 all-gather.14
  632.1 33.1 all-gather.12
  670.1 38.6 reduce-scatter.1
